TPU v7x, 32 devices: a whole 2x2x4 slice. The times are simulated.
32 devices in a mesh: groups: 2 (over y), ctx: 8 (over z, x), head: 2 (over core).
Axes of the slice: x: 2, y: 2, z: 4, core: 2. Of those that a mesh axis runs over, the one named last changes fastest.
Arguments:
- queries: bfloat16 [2048, 2048], P(('groups', 'ctx'), 'head'), parts along dimension 0, may hold values from -16 to 16
- key_states: bfloat16 [2048, 1024], P(('groups', 'ctx'), 'head'), parts along dimension 0, may hold values from -16 to 16
- value_states: bfloat16 [2048, 1024], P(('groups', 'ctx'), 'head'), parts along dimension 0, may hold values from -6 to 6
- out_grad: bfloat16 [2048, 2048], P(('groups', 'ctx'), 'head'), parts along dimension 0, may hold values from -6 to 6
- doc_ids: int32 [32], P('groups'), parts along dimension 0, may hold values from 0 to 5, never falling along the last dimension, each value on 1 to 8 neighbouring positions
- int_pos: int32 [128], P('groups'), parts along dimension 0, may hold values from 0 to 127, as said below
- hidden: bfloat16 [128, 4608], P('groups', 'ctx'), parts along dimension 0, may hold values from -6 to 6
- upstream: bfloat16 [128, 4608], P('groups', 'ctx'), parts along dimension 0, may hold values from -3 to 3
- w_query: bfloat16 [4608, 2048], P('ctx', 'head'), may hold values from -0.09375 to 0.09375
- w_key: bfloat16 [4608, 1024], P('ctx', 'head'), may hold values from -0.09375 to 0.09375
- w_value: bfloat16 [4608, 1024], P('ctx', 'head'), may hold values from -0.09375 to 0.09375
- rotation: float32 [8, 4608], P(None, 'ctx'), may hold values from -0.09375 to 0.09375
- projection: float32 [8, 4608], P(None, 'ctx'), may hold values from -0.09375 to 0.09375
- rank_bias: float32 [8], replicated, may hold values from -4 to 4
Outputs:
- grad_rot: float32 [16, 4608], P('groups', 'ctx'), parts along dimension 0
- grad_proj: float32 [16, 4608], P('groups', 'ctx'), parts along dimension 0
- grad_bias: float32 [16], P('groups'), parts along dimension 0
There are 2 independent parts, one for each index of `groups`. A program takes and returns all parts, laid end to end along the dimension named above; an argument that names none is the same for every part. Nothing has to cross between parts.
Inputs may be any that keep to these rules, and one draw needn't show every extreme that they name: `doc_ids`: ids never fall along the blocks; each document covers 1 to 8 consecutive blocks, and one covers exactly 8. `int_pos`: each aligned group of 8 entries belongs to one block of 128 tokens and holds distinct token indices inside that block in rising order.
All inputs are finite; a program needn't handle non-finite values.
Results may differ from a plain program's by a relative error of at most 0.004.
The roundings to bfloat16 on the way count: a program that leaves them out, or rounds other values in their place, can miss the bound.
Values may be sent and summed in bfloat16 or wider, within the bound.
A program may use at most 64 MiB of HBM per device.

v0:
```python
import jax
import jax.numpy as jnp
from jax import lax
from jax.sharding import PartitionSpec as P

HD = 128
BLK = 64
POS_DEV = 8
scale_q = 1.0 / 12.0
soft_cap = 50.0
key_block = 512


def capping(dot_vals):
    return soft_cap * jnp.tanh(dot_vals * scale_q / soft_cap)


def doc_lookup(doc_table, block_idx):
    table_ids = jnp.arange(doc_table.shape[0], dtype=jnp.int32)
    return jnp.sum(
        jnp.where(block_idx[:, None] == table_ids[None, :], doc_table[None, :], 0), axis=1
    )


def local(
    queries,
    key_states,
    value_states,
    out_grad,
    doc_ids,
    int_pos,
    hidden,
    upstream,
    w_query,
    w_key,
    w_value,
    rotation,
    projection,
    rank_bias,
):
    tokens = queries.shape[0]
    kv_width = key_states.shape[1]
    groups_kv = kv_width // HD
    per_group = queries.shape[1] // kv_width
    pick_count = POS_DEV
    ctx_index = lax.axis_index("ctx")
    my_pos = lax.dynamic_slice_in_dim(int_pos, ctx_index * pick_count, pick_count, 0)
    query_pos = ctx_index * tokens + jnp.arange(tokens, dtype=jnp.int32)
    query_doc = doc_lookup(doc_ids, query_pos // BLK)
    pick_pos = ctx_index * tokens + my_pos
    pick_doc = doc_lookup(doc_ids, pick_pos // BLK)
    query_heads = queries.reshape(tokens, groups_kv, per_group, HD)
    grad_heads = out_grad.reshape(tokens, groups_kv, per_group, HD)
    pick_query = jnp.take(queries, my_pos, axis=0).reshape(pick_count, groups_kv, per_group, HD)
    pick_grad = jnp.take(out_grad, my_pos, axis=0).reshape(pick_count, groups_kv, per_group, HD)

    def visit_keys(running, kv_rows, first_row):
        z_total, numerator, main_sum, side_sum = running
        row_count = kv_rows.shape[0]
        key_pos = first_row + jnp.arange(row_count, dtype=jnp.int32)
        key_doc = doc_lookup(doc_ids, key_pos // BLK)
        key_heads = kv_rows[:, :kv_width].reshape(row_count, groups_kv, HD)
        value_heads = kv_rows[:, kv_width:].reshape(row_count, groups_kv, HD)
        capped = capping(
            jnp.einsum("tgqd,rgd->gqtr", query_heads, key_heads, preferred_element_type=jnp.float32)
        )
        visible = (
            (key_pos[None, :] <= query_pos[:, None])
            & (key_doc[None, :] == query_doc[:, None])
            & (key_pos[None, :] >= 0)
        )
        weights = jnp.where(visible, jnp.exp(capped), 0.0)
        z_total = z_total + jnp.sum(weights, axis=-1)
        numerator = numerator + jnp.einsum(
            "gqtr,rgd->tgqd",
            weights.astype(jnp.bfloat16),
            value_heads,
            preferred_element_type=jnp.float32,
        )
        pick_capped = capping(
            jnp.einsum("pgqd,rgd->gqpr", pick_query, key_heads, preferred_element_type=jnp.float32)
        )
        pick_visible = (
            (key_pos[None, :] <= pick_pos[:, None])
            & (key_doc[None, :] == pick_doc[:, None])
            & (key_pos[None, :] >= 0)
        )
        pick_weights = jnp.where(
            pick_visible, jnp.exp(pick_capped) * (1.0 - (pick_capped / soft_cap) ** 2), 0.0
        )
        prob_grad = jnp.einsum(
            "pgqd,rgd->gqpr", pick_grad, value_heads, preferred_element_type=jnp.float32
        )
        main_sum = main_sum + jnp.einsum(
            "gqpr,rgd->pgqd",
            (pick_weights * prob_grad).astype(jnp.bfloat16),
            key_heads,
            preferred_element_type=jnp.float32,
        )
        side_sum = side_sum + jnp.einsum(
            "gqpr,rgd->pgqd",
            pick_weights.astype(jnp.bfloat16),
            key_heads,
            preferred_element_type=jnp.float32,
        )
        return (z_total, numerator, main_sum, side_sum)

    kv_local = jnp.concatenate([key_states, value_states], axis=1)
    start_state = (
        jnp.zeros((groups_kv, per_group, tokens), jnp.float32),
        jnp.zeros((tokens, groups_kv, per_group, HD), jnp.float32),
        jnp.zeros((pick_count, groups_kv, per_group, HD), jnp.float32),
        jnp.zeros((pick_count, groups_kv, per_group, HD), jnp.float32),
    )
    running = start_state
    kv_piece = lax.all_gather(kv_local, "ctx", axis=0, tiled=True)
    row_count = kv_piece.shape[0]

    def one_block(accum_state, block_no):
        block_rows = lax.dynamic_slice_in_dim(kv_piece, block_no * key_block, key_block, 0)
        return (visit_keys(accum_state, block_rows, block_no * key_block), None)

    running, _ = lax.scan(one_block, running, jnp.arange(row_count // key_block, dtype=jnp.int32))
    z_total, numerator, main_sum, side_sum = running
    z_tok = jnp.transpose(z_total, (2, 0, 1))
    outputs = numerator / z_tok[..., None]
    row_delta = jnp.sum(grad_heads.astype(jnp.float32) * outputs, axis=-1)
    pick_z = jnp.take(z_tok, my_pos, axis=0)
    pick_delta = jnp.take(row_delta, my_pos, axis=0)
    dq_rows = (
        (scale_q * (main_sum - pick_delta[..., None] * side_sum) / pick_z[..., None])
        .reshape(pick_count, queries.shape[1])
        .astype(jnp.bfloat16)
    )
    delta_heads = jnp.transpose(row_delta, (1, 2, 0))
    picked = jnp.concatenate(
        [jnp.take(key_states, my_pos, axis=0), jnp.take(value_states, my_pos, axis=0)], axis=1
    )
    gathered = lax.all_gather(picked, "ctx", axis=0, tiled=True)
    block_rows = gathered
    row_ids = jnp.arange(pick_count * lax.axis_size("ctx"), dtype=jnp.int32)
    key_pos = row_ids // pick_count * tokens + int_pos
    row_count = block_rows.shape[0]
    key_doc = doc_lookup(doc_ids, key_pos // BLK)
    key_heads = block_rows[:, :kv_width].reshape(row_count, groups_kv, HD)
    value_heads = block_rows[:, kv_width:].reshape(row_count, groups_kv, HD)
    capped = capping(
        jnp.einsum("tgqd,rgd->gqtr", query_heads, key_heads, preferred_element_type=jnp.float32)
    )
    visible = (key_pos[None, :] <= query_pos[:, None]) & (key_doc[None, :] == query_doc[:, None])
    probs = jnp.where(visible, jnp.exp(capped), 0.0) / z_total[..., None]
    prob_grad = jnp.einsum(
        "tgqd,rgd->gqtr", grad_heads, value_heads, preferred_element_type=jnp.float32
    )
    dscore = probs * (prob_grad - delta_heads[..., None]) * (1.0 - (capped / soft_cap) ** 2)
    value_grad = jnp.einsum(
        "gqtr,tgqd->rgd", probs.astype(jnp.bfloat16), grad_heads, preferred_element_type=jnp.float32
    )
    key_grad = scale_q * jnp.einsum(
        "gqtr,tgqd->rgd",
        dscore.astype(jnp.bfloat16),
        query_heads,
        preferred_element_type=jnp.float32,
    )
    key_sums = lax.psum_scatter(
        jnp.concatenate(
            [key_grad.reshape(row_count, kv_width), value_grad.reshape(row_count, kv_width)], axis=1
        ),
        "ctx",
        scatter_dimension=0,
        tiled=True,
    )
    pos_rows = jnp.concatenate([dq_rows, key_sums.astype(jnp.bfloat16)], axis=1)
    weight_cat = jnp.concatenate([w_query, w_key, w_value], axis=1)
    partial_grad = lax.dot_general(
        lax.all_gather(pos_rows, "ctx", axis=0, tiled=True),
        weight_cat,
        (((1,), (1,)), ((), ())),
        preferred_element_type=jnp.float32,
    )
    resid_grad = lax.psum(partial_grad, "head") + upstream.astype(jnp.float32)
    hidden_wide = hidden.astype(jnp.float32)
    rank_part = jnp.dot(resid_grad, rotation.T, precision=lax.Precision.HIGHEST)
    state_part = jnp.dot(hidden_wide, (projection - rotation).T, precision=lax.Precision.HIGHEST)
    rank_grad, rank_state = lax.psum((rank_part, state_part), "ctx")
    rank_state = rank_state + rank_bias[None, :]
    grad_bias = jnp.sum(rank_grad, axis=0)
    grad_proj = jnp.dot(rank_grad.T, hidden_wide, precision=lax.Precision.HIGHEST)
    grad_rot = jnp.dot(rank_state.T, resid_grad, precision=lax.Precision.HIGHEST) - grad_proj
    return (grad_rot, grad_proj, grad_bias)


def solution(mesh):
    in_specs = (
        P(("groups", "ctx"), "head"),
        P(("groups", "ctx"), "head"),
        P(("groups", "ctx"), "head"),
        P(("groups", "ctx"), "head"),
        P("groups"),
        P("groups"),
        P("groups", "ctx"),
        P("groups", "ctx"),
        P("ctx", "head"),
        P("ctx", "head"),
        P("ctx", "head"),
        P(None, "ctx"),
        P(None, "ctx"),
        P(),
    )
    out_specs = (P("groups", "ctx"), P("groups", "ctx"), P("groups"))
    return jax.shard_map(local, mesh=mesh, in_specs=in_specs, out_specs=out_specs, check_vma=False)
```

profile of v0, /device:TPU:0, one launch (start us, length us, event | category | flops | bytes accessed | tf_op | source)
XLA Modules:
  0.0 219.9 jit_solution(13700051381468569167)
XLA Ops:
  7.3 1.1 copy.98
  8.4 1.0 copy.99
  9.4 0.7 pad_maximum_fusion
  10.3 1.1 copy.100
  11.4 0.7 compare_and_fusion.1
  12.1 1.6 gather_fusion
  13.7 0.6 gather_fusion.1
  14.3 0.2 copy.102
  14.5 0.6 gather_fusion.4
  15.1 0.6 gather_fusion.5
  15.6 0.2 copy.101
  15.9 32.5 %all_gather.10 = bf16[64,1024]{1,0:T(8,128)(2,1)S(1)} all-gather(bf16[8,1024]{1,0:T(8,128)(2,1)S(1)} %pad_maximum_fusion.3), channel_id=1, replica_groups=mesh['groups'=2,'ctx'=8,'head'=2] {'ctx'}, dimensions={0}, use_global_device_ids=true | all-gather | bytes 147456 | tf_op jit(solution)/shard_map/all_gather | solution.py:139
  48.5 0.1 and_select_fusion.2
  48.6 0.2 select_reduce_fusion.3
  48.8 0.1 select_reduce_fusion.2
  48.9 0.1 select_reduce_fusion.1
  49.0 0.1 compare_and_fusion
  49.1 0.1 broadcast_select_fusion
  49.2 0.2 fusion.22
  49.4 15.3 %all-gather.2.cloned.1.call-done = bf16[1024,1024]{0,1:T(8,128)(2,1)} async-done(((bf16[128,1024]{0,1:T(8,128)(2,1)}), bf16[1024,1024]{0,1:T(8,128)(2,1)}) %all-gather.2.cloned.1.call-update) | async-done | bytes 2097168 | tf_op jit(solution)/shard_map/all_gather | solution.py:116
  64.7 10.2 %while.20 = (s32[]{:T(128)}, f32[4,2,128]{2,1,0:T(2,128)S(1)}, f32[128,4,2,128]{0,3,2,1:T(8,128)S(1)}, f32[8,4,2,128]{3,0,2,1:T(8,128)S(1)}, f32[8,4,2,128]{3,0,...) while((s32[]{:T(128)}, f32[4,2,128]{2,1,0:T(2,128)S(1)}, ...), condition=%wide.region_6.8_spmd.clone, body=%wide.region_3.7_spmd.clone.sunk | while | flops 305514112 | bytes 9383324 | solution.py:123
  64.7 0.6 dynamic_slice.26
  65.9 0.1 select_reduce_fusion.5
  66.0 0.1 and_and_fusion.5
  66.1 1.3 fusion.113
  67.4 0.2 bitcast_select_fusion.4
  67.6 0.3 fusion.117
  67.9 0.3 and_and_fusion.4
  68.2 0.9 fusion.115
  69.1 0.4 fusion.116
  69.5 0.2 fusion.118
  69.8 0.6 dynamic_slice.26
  71.0 0.1 select_reduce_fusion.5
  71.1 0.1 and_and_fusion.5
  71.2 1.3 fusion.113
  72.5 0.2 bitcast_select_fusion.4
  72.7 0.3 fusion.117
  73.0 0.3 and_and_fusion.4
  73.3 0.9 fusion.115
  74.2 0.4 fusion.116
  74.6 0.2 fusion.118
  74.9 0.1 multiply_reduce_fusion
  75.0 0.2 convolution_bitcast_fusion.4
  75.2 0.3 fusion.28
  75.6 0.7 pad_maximum_fusion.1
  76.3 0.2 copy.105
  76.5 0.2 copy.103
  76.7 0.6 gather_fusion.2
  77.2 0.6 gather_fusion.3
  77.8 0.1 broadcast_select_fusion.3
  77.9 0.1 copy.106
  78.0 0.1 copy.107
  78.1 0.1 divide_convert_fusion
  78.2 57.9 %reduce-scatter.2.cloned.1.call-done = f32[8,1024]{1,0:T(8,128)} async-done(((f32[64,1024]{1,0:T(8,128)}), f32[8,1024]{1,0:T(8,128)}) %reduce-scatter.2.cloned.1.call-update) | async-done | bytes 32784 | tf_op jit(solution)/shard_map/reduce_scatter | solution.py:165
  136.1 0.8 convert_element_type.48
  136.8 30.9 %all_gather.11 = bf16[64,2048]{1,0:T(8,128)(2,1)S(1)} all-gather(bf16[8,2048]{1,0:T(8,128)(2,1)S(1)} %pad_maximum_fusion.2), channel_id=1, replica_groups=mesh['groups'=2,'ctx'=8,'head'=2] {'ctx'}, dimensions={0}, use_global_device_ids=true | all-gather | bytes 294912 | tf_op jit(solution)/shard_map/all_gather | solution.py:176
  167.8 2.8 %fusion.16 = f32[64,576]{1,0:T(8,128)} fusion(bf16[64,2048]{1,0:T(8,128)(2,1)S(1)} %all_gather.11, bf16[576,512]{1,0:T(8,128)(2,1)} %param.32, bf16[576,512]{1,0:T(8,128)(2,1)} %param.31, bf16[576,1024]{1,0:T(8,128)(2,1)S(1)} %copy-done.11), kind=kOutput, calls=%fused_computation.40 | convolution fusion | flops 158072832 | bytes 2768896 | tf_op jit(solution)/shard_map/dot_general | solution.py:175
  170.6 0.1 convolution_bitcast_fusion.6
  170.7 17.0 %all-reduce.3.cloned.1.call-done = f32[64,576]{1,0:T(8,128)} async-done(((f32[64,576]{1,0:T(8,128)}), f32[64,576]{1,0:T(8,128)}) %all-reduce.3.cloned.1.call-update) | async-done | bytes 147472 | tf_op jit(solution)/shard_map/psum | solution.py:181
  187.8 1.1 fusion.46
  188.9 21.9 %all-reduce = (f32[64,8]{0,1:T(8,128)S(1)}, f32[64,8]{0,1:T(8,128)S(1)}) all-reduce(f32[64,8]{0,1:T(8,128)S(1)} %fusion.46, f32[64,8]{0,1:T(8,128)S(1)} %convolution_bitcast_fusion.6), channel_id=1, replica_groups=mesh['groups'=2,'ctx'=8,'head'=2] {'ctx'}, use_global_device_ids=true, to_apply=%region_11.15 | all-reduce | flops 1024 | bytes 8192 | tf_op jit(solution)/shard_map/psum | solution.py:185
  210.8 0.1 fusion.65
  211.0 0.6 reduce_sum.75
  211.6 1.8 convolution_subtract_fusion
  (54 shorter events, 0.5 us)
Async XLA Ops:
  7.2 163.4 %copy-start = (bf16[64,576]{1,0:T(8,128)(2,1)S(1)}, bf16[64,576]{1,0:T(8,128)(2,1)}, u32[]{:S(2)}) copy-start(bf16[64,576]{1,0:T(8,128)(2,1)} %param.28) | copy-start | bytes 221188
  7.2 7.3 %copy-start.3 = (bf16[128,512]{1,0:T(8,128)(2,1)S(1)}, bf16[128,512]{1,0:T(8,128)(2,1)}, u32[]{:S(2)}) copy-start(bf16[128,512]{1,0:T(8,128)(2,1)} %param.23) | copy-start | bytes 393220
  7.2 7.9 %copy-start.4 = (bf16[128,512]{1,0:T(8,128)(2,1)S(1)}, bf16[128,512]{1,0:T(8,128)(2,1)}, u32[]{:S(2)}) copy-start(bf16[128,512]{1,0:T(8,128)(2,1)} %param.24) | copy-start | bytes 393220
  7.2 41.3 %copy-start.9 = (s32[64]{0:T(128)S(1)}, s32[64]{0:T(128)}, u32[]{:S(2)}) copy-start(s32[64]{0:T(128)} %param.27) | copy-start | bytes 772
  7.2 6.5 %copy-start.1 = (bf16[128,1024]{1,0:T(8,128)(2,1)S(1)}, bf16[128,1024]{1,0:T(8,128)(2,1)}, u32[]{:S(2)}) copy-start(bf16[128,1024]{1,0:T(8,128)(2,1)} %param.25) | copy-start | bytes 786436
  7.2 41.4 %copy-start.8 = (s32[16]{0:T(128)S(1)}, s32[16]{0:T(128)}, u32[]{:S(2)}) copy-start(s32[16]{0:T(128)} %param.26) | copy-start | bytes 196
  7.2 57.4 %all-gather.2.cloned.1.call-start = ((), (), s32[]{:S(2)}) async-start(), calls=%async_computation.1 | async-start | bytes 2359296 | tf_op jit(solution)/shard_map/all_gather | solution.py:116
  10.2 125.9 %reduce-scatter.2.cloned.1.call-start = ((), (), s32[]{:S(2)}) async-start(), calls=%async_computation.2 | async-start | bytes 294912 | tf_op jit(solution)/shard_map/reduce_scatter | solution.py:165
  75.2 92.6 %copy-start.11 = (bf16[576,1024]{1,0:T(8,128)(2,1)S(1)}, bf16[576,1024]{1,0:T(8,128)(2,1)}, u32[]{:S(2)}) copy-start(bf16[576,1024]{1,0:T(8,128)(2,1)} %param.30) | copy-start | bytes 3538948
  76.3 111.5 %all-reduce.3.cloned.1.call-start = ((), (), s32[]{:S(2)}) async-start(), calls=%async_computation.3 | async-start | bytes 327680 | tf_op jit(solution)/shard_map/psum | solution.py:181
  167.8 2.8 %copy-start.5 = (f32[8,576]{1,0:T(8,128)S(1)}, f32[8,576]{1,0:T(8,128)}, u32[]{:S(2)}) copy-start(f32[8,576]{1,0:T(8,128)} %param.33) | copy-start | bytes 55300
  167.8 2.9 %copy-start.7 = (f32[8,576]{1,0:T(8,128)S(1)}, f32[8,576]{1,0:T(8,128)}, u32[]{:S(2)}) copy-start(f32[8,576]{1,0:T(8,128)} %param.34) | copy-start | bytes 55300
  167.8 20.0 %copy-start.2 = (bf16[64,576]{1,0:T(8,128)(2,1)S(1)}, bf16[64,576]{1,0:T(8,128)(2,1)}, u32[]{:S(2)}) copy-start(bf16[64,576]{1,0:T(8,128)(2,1)} %param.29) | copy-start | bytes 221188
  167.8 43.8 %copy-start.10 = (f32[8]{0:T(128)S(1)}, f32[8]{0:T(128)}, u32[]{:S(2)}) copy-start(f32[8]{0:T(128)} %param.35) | copy-start | bytes 100
  211.0 2.4 %copy-start.6 = (f32[8,576]{1,0:T(8,128)}, f32[8,576]{1,0:T(8,128)S(1)}, u32[]{:S(2)}) copy-start(f32[8,576]{1,0:T(8,128)S(1)} %fusion.65) | copy-start | bytes 55300
Sparse Core Ops, SparseCore 0:
  10.3 54.3 all-gather.1
  76.4 59.6 reduce-scatter.1
  170.7 17.0 all-reduce.2
where the time goes:
time: 220 us
  waiting for transfers between devices  90.3 us (41%)
  blocking collectives  85.3 us (39%)
  between operations  14.1 us (6%)
  local copies, waits for them, and re-layouts  12.4 us (6%)
  matrix products  10.7 us (5%)
  other arithmetic  5.58 us (3%)
    reduce_scatter x1, waiting for transfers between devices, local(): lax.psum_scatter(jnp.concatenate([key_grad.reshape(row_count, kv_width),...  57.9 us
    all_gather x1, blocking collectives, local(): gathered = lax.all_gather(picked, 'ctx', axis=0, tiled=True)  32.5 us
    all_gather x1, blocking collectives, local(): lax.all_gather(pos_rows, 'ctx', axis=0, tiled=True)  30.9 us
    psum x1, blocking collectives, local(): rank_grad, rank_state = lax.psum((rank_part, state_part), 'ctx')  21.9 us
    psum x1, waiting for transfers between devices, local(): resid_grad = lax.psum(partial_grad, 'head') + upstream.astype(jnp.float32)  17 us
    all_gather x1, waiting for transfers between devices, local(): kv_piece = lax.all_gather(kv_local, 'ctx', axis=0, tiled=True)  15.3 us
  transfers between devices with their start and end apart: 3, of which 3 were waited for; matrix products, arithmetic and copies ran while one was open for 4% of the time, Pallas kernels for 0%

commit v1 on v0

--- a/solution.py
+++ b/solution.py
@@ -178,7 +178,9 @@
         (((1,), (1,)), ((), ())),
         preferred_element_type=jnp.float32,
     )
-    resid_grad = lax.psum(partial_grad, "head") + upstream.astype(jnp.float32)
+    resid_grad = jnp.sum(lax.all_gather(partial_grad, "head"), axis=0) + upstream.astype(
+        jnp.float32
+    )
     hidden_wide = hidden.astype(jnp.float32)
     rank_part = jnp.dot(resid_grad, rotation.T, precision=lax.Precision.HIGHEST)
     state_part = jnp.dot(hidden_wide, (projection - rotation).T, precision=lax.Precision.HIGHEST)

time: 220 us -> 201 us (0.914)
  waiting for transfers between devices: 90.3 us -> 73 us
  matrix products: 10.7 us -> 8 us
    psum x1 -> x0, waiting for transfers between devices: 17 us -> none  [local(): resid_grad = lax.psum(partial_grad, 'head') + upstream.astype(jnp.float32)]
  transfers between devices with their start and end apart: 3 -> 2, of which waited for: 3 -> 2; matrix products, arithmetic and copies ran while one was open for 4% -> 4% of each run, Pallas kernels for 0% -> 0%
where the time goes in v1:
time: 201 us; the launch traced here: 200 us
  blocking collectives  85.2 us (42%)
  waiting for transfers between devices  73 us (36%)
  between operations  14.4 us (7%)
  local copies, waits for them, and re-layouts  12.5 us (6%)
  matrix products  8 us (4%)
  other arithmetic  5.61 us (3%)
    reduce_scatter x1, waiting for transfers between devices, local(): lax.psum_scatter(jnp.concatenate([key_grad.reshape(row_count, kv_width),...  57.7 us
    all_gather x1, blocking collectives, local(): gathered = lax.all_gather(picked, 'ctx', axis=0, tiled=True)  32.5 us
    all_gather x1, blocking collectives, local(): lax.all_gather(pos_rows, 'ctx', axis=0, tiled=True)  30.9 us
    psum x1, blocking collectives, local(): rank_grad, rank_state = lax.psum((rank_part, state_part), 'ctx')  19.7 us
    all_gather x1, waiting for transfers between devices, local(): kv_piece = lax.all_gather(kv_local, 'ctx', axis=0, tiled=True)  15.3 us
  transfers between devices with their start and end apart: 2, of which 2 were waited for; matrix products, arithmetic and copies ran while one was open for 4% of the time, Pallas kernels for 0%

profile of v1, /device:TPU:0, one launch (start us, length us, event | category | flops | bytes accessed | tf_op | source)
XLA Modules:
  0.0 200.2 jit_solution(4685221823068516483)
XLA Ops:
  7.3 1.1 copy.98
  8.4 1.0 copy.99
  9.4 0.7 pad_maximum_fusion
  10.3 1.1 copy.100
  11.4 0.7 compare_and_fusion.1
  12.2 1.6 gather_fusion
  13.7 0.6 gather_fusion.1
  14.3 0.2 copy.102
  14.5 0.6 gather_fusion.4
  15.1 0.6 gather_fusion.5
  15.7 0.2 copy.101
  15.9 32.5 %all_gather.16 = bf16[64,1024]{1,0:T(8,128)(2,1)S(1)} all-gather(bf16[8,1024]{1,0:T(8,128)(2,1)S(1)} %pad_maximum_fusion.3), channel_id=1, replica_groups=mesh['groups'=2,'ctx'=8,'head'=2] {'ctx'}, dimensions={0}, use_global_device_ids=true | all-gather | bytes 147456 | tf_op jit(solution)/shard_map/all_gather | solution.py:139
  48.5 0.1 and_select_fusion.2
  48.6 0.2 select_reduce_fusion.3
  48.8 0.1 select_reduce_fusion.2
  48.9 0.1 select_reduce_fusion.1
  49.0 0.1 compare_and_fusion
  49.1 0.1 broadcast_select_fusion
  49.2 0.2 fusion.22
  49.4 15.3 %all-gather.3.cloned.1.call-done = bf16[1024,1024]{0,1:T(8,128)(2,1)} async-done(((bf16[128,1024]{0,1:T(8,128)(2,1)}), bf16[1024,1024]{0,1:T(8,128)(2,1)}) %all-gather.3.cloned.1.call-update) | async-done | bytes 2097168 | tf_op jit(solution)/shard_map/all_gather | solution.py:116
  64.7 10.2 %while.20 = (s32[]{:T(128)}, f32[4,2,128]{2,1,0:T(2,128)S(1)}, f32[128,4,2,128]{0,3,2,1:T(8,128)S(1)}, f32[8,4,2,128]{3,0,2,1:T(8,128)S(1)}, f32[8,4,2,128]{3,0,...) while((s32[]{:T(128)}, f32[4,2,128]{2,1,0:T(2,128)S(1)}, ...), condition=%wide.region_6.8_spmd.clone, body=%wide.region_3.7_spmd.clone.sunk | while | flops 305514112 | bytes 9383324 | solution.py:123
  64.7 0.6 dynamic_slice.26
  65.9 0.1 select_reduce_fusion.5
  66.0 0.1 and_and_fusion.5
  66.1 1.3 fusion.113
  67.4 0.2 bitcast_select_fusion.4
  67.6 0.3 fusion.117
  67.9 0.3 and_and_fusion.4
  68.2 0.9 fusion.115
  69.1 0.4 fusion.116
  69.5 0.2 fusion.118
  69.8 0.6 dynamic_slice.26
  71.0 0.1 select_reduce_fusion.5
  71.1 0.1 and_and_fusion.5
  71.2 1.3 fusion.113
  72.5 0.2 bitcast_select_fusion.4
  72.7 0.3 fusion.117
  73.0 0.3 and_and_fusion.4
  73.3 0.9 fusion.115
  74.2 0.4 fusion.116
  74.6 0.2 fusion.118
  74.9 0.1 multiply_reduce_fusion
  75.0 0.2 convolution_bitcast_fusion.4
  75.2 0.3 fusion.28
  75.6 0.7 pad_maximum_fusion.1
  76.4 0.1 convolution_bitcast_fusion.6
  76.5 0.2 copy.105
  76.7 0.2 copy.103
  76.9 0.6 gather_fusion.2
  77.5 0.6 gather_fusion.3
  78.0 0.1 broadcast_select_fusion.3
  78.1 0.1 copy.106
  78.2 0.1 copy.107
  78.3 0.1 divide_convert_fusion
  78.4 57.7 %reduce-scatter.2.cloned.1.call-done = f32[8,1024]{1,0:T(8,128)} async-done(((f32[64,1024]{1,0:T(8,128)}), f32[8,1024]{1,0:T(8,128)}) %reduce-scatter.2.cloned.1.call-update) | async-done | bytes 32784 | tf_op jit(solution)/shard_map/reduce_scatter | solution.py:165
  136.1 0.8 convert_element_type.48
  136.9 30.9 %all_gather.17 = bf16[64,2048]{1,0:T(8,128)(2,1)S(1)} all-gather(bf16[8,2048]{1,0:T(8,128)(2,1)S(1)} %pad_maximum_fusion.2), channel_id=1, replica_groups=mesh['groups'=2,'ctx'=8,'head'=2] {'ctx'}, dimensions={0}, use_global_device_ids=true | all-gather | bytes 294912 | tf_op jit(solution)/shard_map/all_gather | solution.py:176
  167.8 1.9 fusion.16
  169.7 2.0 %all-gather = f32[128,576]{1,0:T(8,128)S(1)} all-gather(f32[64,576]{1,0:T(8,128)S(1)} %fusion.16), channel_id=2, replica_groups=mesh['groups'=2,'ctx'=8,'head'=2] {'head'}, dimensions={0}, use_global_device_ids=true | all-gather | bytes 442368 | tf_op jit(solution)/shard_map/all_gather | solution.py:181
  171.8 0.2 fusion.46
  172.0 19.7 %all-reduce = (f32[64,8]{0,1:T(8,128)S(1)}, f32[64,8]{0,1:T(8,128)S(1)}) all-reduce(f32[64,8]{0,1:T(8,128)S(1)} %fusion.46, f32[64,8]{0,1:T(8,128)S(1)} %convolution_bitcast_fusion.6), channel_id=1, replica_groups=mesh['groups'=2,'ctx'=8,'head'=2] {'ctx'}, use_global_device_ids=true, to_apply=%region_11.15 | all-reduce | flops 1024 | bytes 8192 | tf_op jit(solution)/shard_map/psum | solution.py:187
  191.7 0.1 fusion.65
  191.9 0.6 reduce_sum.85
  192.5 0.9 convolution_subtract_fusion
  (55 shorter events, 0.5 us)
Async XLA Ops:
  7.2 69.2 %copy-start = (bf16[64,576]{1,0:T(8,128)(2,1)S(1)}, bf16[64,576]{1,0:T(8,128)(2,1)}, u32[]{:S(2)}) copy-start(bf16[64,576]{1,0:T(8,128)(2,1)} %param.28) | copy-start | bytes 221188
  7.2 7.3 %copy-start.3 = (bf16[128,512]{1,0:T(8,128)(2,1)S(1)}, bf16[128,512]{1,0:T(8,128)(2,1)}, u32[]{:S(2)}) copy-start(bf16[128,512]{1,0:T(8,128)(2,1)} %param.23) | copy-start | bytes 393220
  7.2 7.9 %copy-start.4 = (bf16[128,512]{1,0:T(8,128)(2,1)S(1)}, bf16[128,512]{1,0:T(8,128)(2,1)}, u32[]{:S(2)}) copy-start(bf16[128,512]{1,0:T(8,128)(2,1)} %param.24) | copy-start | bytes 393220
  7.2 41.3 %copy-start.9 = (s32[64]{0:T(128)S(1)}, s32[64]{0:T(128)}, u32[]{:S(2)}) copy-start(s32[64]{0:T(128)} %param.27) | copy-start | bytes 772
  7.2 6.5 %copy-start.1 = (bf16[128,1024]{1,0:T(8,128)(2,1)S(1)}, bf16[128,1024]{1,0:T(8,128)(2,1)}, u32[]{:S(2)}) copy-start(bf16[128,1024]{1,0:T(8,128)(2,1)} %param.25) | copy-start | bytes 786436
  7.2 41.4 %copy-start.8 = (s32[16]{0:T(128)S(1)}, s32[16]{0:T(128)}, u32[]{:S(2)}) copy-start(s32[16]{0:T(128)} %param.26) | copy-start | bytes 196
  7.2 57.4 %all-gather.3.cloned.1.call-start = ((), (), s32[]{:S(2)}) async-start(), calls=%async_computation.1 | async-start | bytes 2359296 | tf_op jit(solution)/shard_map/all_gather | solution.py:116
  10.2 125.9 %reduce-scatter.2.cloned.1.call-start = ((), (), s32[]{:S(2)}) async-start(), calls=%async_computation.2 | async-start | bytes 294912 | tf_op jit(solution)/shard_map/reduce_scatter | solution.py:165
  75.0 1.4 copy-start.5
  75.0 1.4 copy-start.7
  75.2 92.5 %copy-start.11 = (bf16[576,1024]{1,0:T(8,128)(2,1)S(1)}, bf16[576,1024]{1,0:T(8,128)(2,1)}, u32[]{:S(2)}) copy-start(bf16[576,1024]{1,0:T(8,128)(2,1)} %param.30) | copy-start | bytes 3538948
  75.6 92.2 %copy-start.12 = (bf16[576,512]{1,0:T(8,128)(2,1)S(1)}, bf16[576,512]{1,0:T(8,128)(2,1)}, u32[]{:S(2)}) copy-start(bf16[576,512]{1,0:T(8,128)(2,1)} %param.32) | copy-start | bytes 1769476
  167.8 4.0 %copy-start.2 = (bf16[64,576]{1,0:T(8,128)(2,1)S(1)}, bf16[64,576]{1,0:T(8,128)(2,1)}, u32[]{:S(2)}) copy-start(bf16[64,576]{1,0:T(8,128)(2,1)} %param.29) | copy-start | bytes 221188
  167.8 24.7 %copy-start.10 = (f32[8]{0:T(128)S(1)}, f32[8]{0:T(128)}, u32[]{:S(2)}) copy-start(f32[8]{0:T(128)} %param.35) | copy-start | bytes 100
  191.9 1.5 copy-start.6
Sparse Core Ops, SparseCore 0:
  10.3 54.3 all-gather.2
  76.5 59.6 reduce-scatter.1
